TPU v7x, 32 devices: a whole 2x2x4 slice. The times are simulated.
32 devices in a mesh: shard: 4 (over y, x), ctx: 8 (over z, core).
Axes of the slice: x: 2, y: 2, z: 4, core: 2. Of those that a mesh axis runs over, the one named last changes fastest.
Arguments:
- tokens: bfloat16 [4, 1024, 768], P('shard', 'ctx'), may hold values from -60 to 60
- lengths: int32 [4], P('shard'), may hold values from 128 to 1024, as said below
- cotangent: bfloat16 [4, 1024, 768], P('shard', 'ctx'), may hold values from -6 to 6
- w_qkv: bfloat16 [768, 2304], P('shard'), may hold values from -0.21875 to 0.21875
- b_query: bfloat16 [768], P('shard'), may hold values from -3 to 3
- b_value: bfloat16 [768], P('shard'), may hold values from -3 to 3
- w_out: bfloat16 [768, 768], P('shard'), may hold values from -3.5 to 3.5
- b_out: bfloat16 [768], P('shard'), may hold values from -3 to 3
- ln1_gain: bfloat16 [768], P('shard'), may hold values from 0.25 to 1.75
- ln1_bias: bfloat16 [768], P('shard'), may hold values from -3 to 3
- w_up: bfloat16 [768, 3072], P('shard'), may hold values from -0.21875 to 0.21875
- b_up: bfloat16 [3072], P('shard'), may hold values from -3 to 3
- w_down: bfloat16 [3072, 768], P('shard'), may hold values from -0.109375 to 0.109375
- b_down: bfloat16 [768], P('shard'), may hold values from -3 to 3
- ln2_gain: bfloat16 [768], P('shard'), may hold values from 0.25 to 1.75
- ln2_bias: bfloat16 [768], P('shard'), may hold values from -3 to 3
Outputs:
- output: bfloat16 [4, 1024, 768], P('shard', 'ctx')
- tokens_grad: float32 [4, 1024, 768], P('shard', 'ctx')
- w_qkv_grad: float32 [768, 2304], P('shard')
- b_query_grad: float32 [768], P('shard')
- b_value_grad: float32 [768], P('shard')
- w_out_grad: float32 [768, 768], P('shard')
- b_out_grad: float32 [768], P('shard')
- ln1_gain_grad: float32 [768], P('shard')
- ln1_bias_grad: float32 [768], P('shard')
- w_up_grad: float32 [768, 3072], P('shard')
- b_up_grad: float32 [3072], P('shard')
- w_down_grad: float32 [3072, 768], P('shard')
- b_down_grad: float32 [768], P('shard')
- ln2_gain_grad: float32 [768], P('shard')
- ln2_bias_grad: float32 [768], P('shard')
Inputs may be any that keep to these rules, and one draw needn't show every extreme that they name: `lengths`: each sequence has at least one valid token; some sequence is entirely valid.
All inputs are finite; a program needn't handle non-finite values.
Results may differ from a plain program's by a relative error of at most 0.035.
The roundings to bfloat16 on the way count: a program that leaves them out, or rounds other values in their place, can miss the bound.
Values may be sent and summed in bfloat16 or wider, within the bound.
A program may use at most 128 MiB of HBM per device.

v0:
```python
import math
import jax
import jax.numpy as jnp
from jax import lax
from jax.sharding import PartitionSpec as P

HEADS = 12
EPS = 1e-06


def normalize(z):
    centre = z - jnp.mean(z, axis=-1, keepdims=True)
    rstd = lax.rsqrt(jnp.mean(centre * centre, axis=-1, keepdims=True) + EPS)
    return (centre * rstd, rstd)


def norm_back(dnorm, normed, rstd):
    return rstd * (
        dnorm
        - jnp.mean(dnorm, axis=-1, keepdims=True)
        - normed * jnp.mean(dnorm * normed, axis=-1, keepdims=True)
    )


def gelu_exact(t):
    return jax.nn.gelu(t, approximate=False)


def contract_dims(left, right, left_dim, right_dim):
    return lax.dot_general(
        left, right, (((left_dim,), (right_dim,)), ((), ())), preferred_element_type=jnp.float32
    )


def heads_first(a):
    return a.reshape(HEADS, a.shape[0] // HEADS, a.shape[1])


def local(
    tokens,
    lengths,
    cotangent,
    w_qkv,
    b_query,
    b_value,
    w_out,
    b_out,
    ln1_gain,
    ln1_bias,
    w_up,
    b_up,
    w_down,
    b_down,
    ln2_gain,
    ln2_bias,
):
    single_float = jnp.float32
    bf16 = jnp.bfloat16
    full = (
        lax.all_gather(w_qkv, "shard", axis=0, tiled=True),
        lax.all_gather(b_query, "shard", axis=0, tiled=True),
        lax.all_gather(b_value, "shard", axis=0, tiled=True),
        lax.all_gather(w_out, "shard", axis=0, tiled=True),
        lax.all_gather(b_out, "shard", axis=0, tiled=True),
        lax.all_gather(ln1_gain, "shard", axis=0, tiled=True),
        lax.all_gather(ln1_bias, "shard", axis=0, tiled=True),
        lax.all_gather(w_up, "shard", axis=0, tiled=True),
        lax.all_gather(b_up, "shard", axis=0, tiled=True),
        lax.all_gather(w_down, "shard", axis=0, tiled=True),
        lax.all_gather(b_down, "shard", axis=0, tiled=True),
        lax.all_gather(ln2_gain, "shard", axis=0, tiled=True),
        lax.all_gather(ln2_bias, "shard", axis=0, tiled=True),
    )
    wq_full, wo_full, wu_full, wd_full = (full[0], full[3], full[7], full[9])
    bq, bv, bo = (
        full[1].astype(single_float),
        full[2].astype(single_float),
        full[4].astype(single_float),
    )
    g1, c1, bu = (
        full[5].astype(single_float),
        full[6].astype(single_float),
        full[8].astype(single_float),
    )
    bd, g2, c2 = (
        full[10].astype(single_float),
        full[11].astype(single_float),
        full[12].astype(single_float),
    )
    x = tokens[0]
    width = x.shape[1]
    head_size = width // HEADS
    scale = 1.0 / math.sqrt(head_size)
    limit = lengths[0]
    qkv_t = contract_dims(wq_full, x, 0, 1)
    query_t = (qkv_t[:width] + bq[:, None]).astype(bf16)
    keys_t = qkv_t[width : 2 * width].astype(bf16)
    values_t = (qkv_t[2 * width :] + bv[:, None]).astype(bf16)
    all_keys, all_values = (
        lax.all_gather(keys_t, "ctx", axis=1, tiled=True),
        lax.all_gather(values_t, "ctx", axis=1, tiled=True),
    )
    total = all_keys.shape[1]
    valid = jnp.arange(total, dtype=jnp.int32) < limit

    def head_fwd(operations):
        query_index, key_index, value_index = operations
        scores = contract_dims(query_index, key_index, 0, 0) * scale
        scores = jnp.where(valid[None, :], scores, -1e30)
        peak = jnp.max(scores, axis=1, keepdims=True)
        lse = peak + jnp.log(jnp.sum(jnp.exp(scores - peak), axis=1, keepdims=True))
        probs = jnp.exp(scores - lse).astype(bf16)
        return (contract_dims(value_index, probs, 1, 1), lse[:, 0])

    ctx_heads, lse_all = lax.map(
        head_fwd, (heads_first(query_t), heads_first(all_keys), heads_first(all_values))
    )
    context_b_t = ctx_heads.reshape(width, -1).astype(bf16)
    z_one = x.astype(single_float) + contract_dims(context_b_t, wo_full, 0, 0) + bo
    n_one, rstd_one = normalize(z_one)
    x_one = n_one * g1 + c1
    x_one_b = x_one.astype(bf16)
    upper = jnp.dot(x_one_b, wu_full, preferred_element_type=single_float) + bu
    hidden_f, gelu_back = jax.vjp(gelu_exact, upper)
    hidden = hidden_f.astype(bf16)
    z_two = x_one + jnp.dot(hidden, wd_full, preferred_element_type=single_float) + bd
    n_two, rstd_two = normalize(z_two)
    out = (n_two * g2 + c2).astype(bf16)
    wq_back, wo_back, wu_back, wd_back = (wq_full, wo_full, wu_full, wd_full)
    keys_b, values_b = (all_keys, all_values)
    grad = cotangent[0].astype(single_float)
    dg_two = jnp.sum(grad * n_two, axis=0)
    db_two = jnp.sum(grad, axis=0)
    dz_two = norm_back(grad * g2, n_two, rstd_two)
    dz_two_b = dz_two.astype(bf16)
    dw_down = contract_dims(hidden, dz_two_b, 0, 0)
    db_down = jnp.sum(dz_two, axis=0)
    dhid = contract_dims(dz_two_b, wd_back, 1, 1)
    dupper = gelu_back(dhid)[0]
    dupper_b = dupper.astype(bf16)
    dw_up = contract_dims(x_one_b, dupper_b, 0, 0)
    db_up = jnp.sum(dupper, axis=0)
    dx_one = dz_two + contract_dims(dupper_b, wu_back, 1, 1)
    dg_one = jnp.sum(dx_one * n_one, axis=0)
    db_one = jnp.sum(dx_one, axis=0)
    dz_one = norm_back(dx_one * g1, n_one, rstd_one)
    dz_one_b = dz_one.astype(bf16)
    dw_out = contract_dims(context_b_t, dz_one_b, 1, 0)
    db_out = jnp.sum(dz_one, axis=0)
    dctx_t = contract_dims(wo_back, dz_one_b, 1, 1)
    dctx_b_t = dctx_t.astype(bf16)
    delta = jnp.sum(heads_first(dctx_t) * ctx_heads, axis=1)
    qh = heads_first(query_t)

    def head_bwd(operations):
        query_index, key_index, value_index, lse_index, context_grad_index, delta_index = operations
        scores = contract_dims(query_index, key_index, 0, 0) * scale
        scores = jnp.where(valid[None, :], scores, -1e30)
        prob = jnp.exp(scores - lse_index[:, None])
        block_probs = prob.astype(bf16)
        value_gradient = contract_dims(context_grad_index, block_probs, 1, 0)
        prob_gradient = contract_dims(context_grad_index, value_index, 0, 0)
        dscore = (prob * (prob_gradient - delta_index[:, None])).astype(bf16)
        query_gradient = contract_dims(key_index, dscore, 1, 1) * scale
        key_gradient = contract_dims(query_index, dscore, 1, 0) * scale
        return (query_gradient, key_gradient, value_gradient)

    dqh, dkh, dvh = lax.map(
        head_bwd,
        (qh, heads_first(keys_b), heads_first(values_b), lse_all, heads_first(dctx_b_t), delta),
    )
    key_grad_t, value_grad_t = (
        lax.psum_scatter(
            dkh.reshape(width, -1).astype(jnp.bfloat16), "ctx", scatter_dimension=1, tiled=True
        ).astype(jnp.float32),
        lax.psum_scatter(
            dvh.reshape(width, -1).astype(jnp.bfloat16), "ctx", scatter_dimension=1, tiled=True
        ).astype(jnp.float32),
    )
    query_grad_t = dqh.reshape(width, -1)
    dqkv_b_t = jnp.concatenate([query_grad_t, key_grad_t, value_grad_t], axis=0).astype(bf16)
    dw_qkv = contract_dims(x, dqkv_b_t, 0, 1)
    dx = dz_one + contract_dims(dqkv_b_t, wq_back, 0, 1)
    grads = (
        dw_qkv,
        jnp.sum(query_grad_t, axis=1),
        jnp.sum(value_grad_t, axis=1),
        dw_out,
        db_out,
        dg_one,
        db_one,
        dw_up,
        db_up,
        dw_down,
        db_down,
        dg_two,
        db_two,
    )
    pieces = (
        lax.psum_scatter(
            grads[0].astype(jnp.bfloat16), "shard", scatter_dimension=0, tiled=True
        ).astype(jnp.float32),
        lax.psum_scatter(
            grads[1].astype(jnp.bfloat16), "shard", scatter_dimension=0, tiled=True
        ).astype(jnp.float32),
        lax.psum_scatter(
            grads[2].astype(jnp.bfloat16), "shard", scatter_dimension=0, tiled=True
        ).astype(jnp.float32),
        lax.psum_scatter(
            grads[3].astype(jnp.bfloat16), "shard", scatter_dimension=0, tiled=True
        ).astype(jnp.float32),
        lax.psum_scatter(
            grads[4].astype(jnp.bfloat16), "shard", scatter_dimension=0, tiled=True
        ).astype(jnp.float32),
        lax.psum_scatter(
            grads[5].astype(jnp.bfloat16), "shard", scatter_dimension=0, tiled=True
        ).astype(jnp.float32),
        lax.psum_scatter(
            grads[6].astype(jnp.bfloat16), "shard", scatter_dimension=0, tiled=True
        ).astype(jnp.float32),
        lax.psum_scatter(
            grads[7].astype(jnp.bfloat16), "shard", scatter_dimension=0, tiled=True
        ).astype(jnp.float32),
        lax.psum_scatter(
            grads[8].astype(jnp.bfloat16), "shard", scatter_dimension=0, tiled=True
        ).astype(jnp.float32),
        lax.psum_scatter(
            grads[9].astype(jnp.bfloat16), "shard", scatter_dimension=0, tiled=True
        ).astype(jnp.float32),
        lax.psum_scatter(
            grads[10].astype(jnp.bfloat16), "shard", scatter_dimension=0, tiled=True
        ).astype(jnp.float32),
        lax.psum_scatter(
            grads[11].astype(jnp.bfloat16), "shard", scatter_dimension=0, tiled=True
        ).astype(jnp.float32),
        lax.psum_scatter(
            grads[12].astype(jnp.bfloat16), "shard", scatter_dimension=0, tiled=True
        ).astype(jnp.float32),
    )
    summed = (
        lax.psum(pieces[0].astype(jnp.bfloat16), "ctx").astype(jnp.float32),
        lax.psum(pieces[1].astype(jnp.bfloat16), "ctx").astype(jnp.float32),
        lax.psum(pieces[2].astype(jnp.bfloat16), "ctx").astype(jnp.float32),
        lax.psum(pieces[3].astype(jnp.bfloat16), "ctx").astype(jnp.float32),
        lax.psum(pieces[4].astype(jnp.bfloat16), "ctx").astype(jnp.float32),
        lax.psum(pieces[5].astype(jnp.bfloat16), "ctx").astype(jnp.float32),
        lax.psum(pieces[6].astype(jnp.bfloat16), "ctx").astype(jnp.float32),
        lax.psum(pieces[7].astype(jnp.bfloat16), "ctx").astype(jnp.float32),
        lax.psum(pieces[8].astype(jnp.bfloat16), "ctx").astype(jnp.float32),
        lax.psum(pieces[9].astype(jnp.bfloat16), "ctx").astype(jnp.float32),
        lax.psum(pieces[10].astype(jnp.bfloat16), "ctx").astype(jnp.float32),
        lax.psum(pieces[11].astype(jnp.bfloat16), "ctx").astype(jnp.float32),
        lax.psum(pieces[12].astype(jnp.bfloat16), "ctx").astype(jnp.float32),
    )
    return (
        out[None],
        dx[None],
        summed[0],
        summed[1],
        summed[2],
        summed[3],
        summed[4],
        summed[5],
        summed[6],
        summed[7],
        summed[8],
        summed[9],
        summed[10],
        summed[11],
        summed[12],
    )


def solution(mesh):
    in_specs = (
        P("shard", "ctx", None),
        P("shard"),
        P("shard", "ctx", None),
        P("shard", None),
        P("shard"),
        P("shard"),
        P("shard", None),
        P("shard"),
        P("shard"),
        P("shard"),
        P("shard", None),
        P("shard"),
        P("shard", None),
        P("shard"),
        P("shard"),
        P("shard"),
    )
    out_specs = (
        P("shard", "ctx", None),
        P("shard", "ctx", None),
        P("shard", None),
        P("shard"),
        P("shard"),
        P("shard", None),
        P("shard"),
        P("shard"),
        P("shard"),
        P("shard", None),
        P("shard"),
        P("shard", None),
        P("shard"),
        P("shard"),
        P("shard"),
    )
    return jax.shard_map(local, mesh=mesh, in_specs=in_specs, out_specs=out_specs, check_vma=False)
```

profile of v0, /device:TPU:0, one launch (start us, length us, event | category | flops | bytes accessed | tf_op | source)
XLA Modules:
  0.0 760.2 jit_solution(821553112586905481)
XLA Ops:
  15.8 18.3 %all-reduce.20 = (bf16[768]{0:T(1024)(128)(2,1)S(1)}, bf16[768]{0:T(1024)(128)(2,1)S(1)}, bf16[768]{0:T(1024)(128)(2,1)S(1)}, bf16[768]{0:T(1024)(128)(2,1)S(1)}...) all-reduce(bf16[768]{0:T(1024)(128)(2,1)S(1)} %dynamic-update-slice, ...), channel_id=1, replica_groups=mesh['shard'=4,'ctx'=8] {'shard'}, use_global_device_ids=true, to_apply=%add.1 | all-reduce | flops 5376 | bytes 21504
  34.1 25.7 %all-gather.8.cloned.1.call-done = bf16[768,2304]{1,0:T(8,128)(2,1)} async-done(((bf16[192,2304]{1,0:T(8,128)(2,1)}), bf16[768,2304]{1,0:T(8,128)(2,1)}) %all-gather.8.cloned.1.call-update) | async-done | bytes 3538960 | tf_op jit(solution)/shard_map/all_gather | solution.py:60
  66.6 8.3 %all-gather = bf16[4,1,768]{2,1,0:T(2,128)(2,1)S(1)} all-gather(bf16[1,1,768]{2,1,0:T(2,128)(2,1)S(1)} %reshape.174), channel_id=1, replica_groups=mesh['shard'=4,'ctx'=8] {'shard'}, dimensions={0}, use_global_device_ids=true | all-gather | bytes 7680 | tf_op jit(solution)/shard_map/all_gather | solution.py:68
  74.9 16.2 %all-gather.10.cloned.1.call-done = bf16[768,1024]{1,0:T(8,128)(2,1)} async-done(((bf16[768,128]{1,0:T(8,128)(2,1)}), bf16[768,1024]{1,0:T(8,128)(2,1)}) %all-gather.10.cloned.1.call-update) | async-done | bytes 1572880 | tf_op jit(solution)/shard_map/all_gather | solution.py:101
  91.2 28.1 %all-gather.12.cloned.1.call-done = bf16[768,1024]{1,0:T(8,128)(2,1)} async-done(((bf16[768,128]{1,0:T(8,128)(2,1)}), bf16[768,1024]{1,0:T(8,128)(2,1)}) %all-gather.12.cloned.1.call-update) | async-done | bytes 1572880 | tf_op jit(solution)/shard_map/all_gather | solution.py:100
  119.3 55.8 %while.28 = (s32[]{:T(128)}, f32[12,64,128]{2,1,0:T(8,128)S(1)}, f32[12,128]{1,0:T(8,128)}, bf16[12,64,1024]{2,1,0:T(8,128)(2,1)}, bf16[12,64,128]{2,1,0:T(8,128...) while((s32[]{:T(128)}, f32[12,64,128]{2,1,0:T(8,128)S(1)}, ...), condition=%wide.region_3.4_spmd.clone, body=%wide.region_0.3_spmd.clone.sunk | while | flops 34472832 | bytes 1892965 | solution.py:115
  177.2 28.8 %all-gather.16.cloned.1.call-done = bf16[768,3072]{1,0:T(8,128)(2,1)} async-done(((bf16[192,3072]{1,0:T(8,128)(2,1)}), bf16[768,3072]{1,0:T(8,128)(2,1)}) %all-gather.16.cloned.1.call-update) | async-done | bytes 4718608 | tf_op jit(solution)/shard_map/all_gather | solution.py:67
  206.0 7.6 %multiply_convert_fusion = (bf16[128,3072]{1,0:T(8,128)(2,1)S(1)}, f32[128,3072]{1,0:T(8,128)}) fusion(f32[3072]{0:T(1024)S(1)} %bitcast.162, bf16[768,3072]{1,0:T(8,128)(2,1)} %all-gather.16.cloned.1.call-done, f32[128,768]{1,0:T(8,128)S(1)} %get-tuple-element.303, f32[768]{0:T(1024)S(1)} %convert_element_type.209, f32[768]{0:T(1024)S(1)} %convert_element_type.208, ...), kind=kOutput, calls=%fused_computation.67 | convolution fusion | flops 630423552 | bytes 7490560 | tf_op jit(solution)/shard_map/dot_general | solution.py:123
  213.7 51.0 %all-gather.18.cloned.1.call-done = bf16[3072,768]{1,0:T(8,128)(2,1)} async-done(((bf16[768,768]{1,0:T(8,128)(2,1)}), bf16[3072,768]{1,0:T(8,128)(2,1)}) %all-gather.18.cloned.1.call-update) | async-done | bytes 4718608 | tf_op jit(solution)/shard_map/all_gather | solution.py:69
  264.7 3.4 fusion.91
  269.9 5.5 fusion.93
  286.0 87.0 %while.29 = (s32[]{:T(128)}, f32[12,64,128]{2,1,0:T(8,128)S(1)}, bf16[12,64,1024]{2,1,0:T(8,128)(2,1)}, bf16[12,64,1024]{2,1,0:T(8,128)(2,1)}, bf16[12,64,1024]{...) while((s32[]{:T(128)}, f32[12,64,128]{2,1,0:T(8,128)S(1)}, ...), condition=%wide.region_14.15_spmd.clone, body=%wide.region_13.14_spmd.clone.sunk | while | flops 84878336 | bytes 3385469 | solution.py:168
  379.3 30.6 %reduce-scatter.19.cloned.1.call-done = bf16[128,768]{1,0:T(8,128)(2,1)} async-done(((bf16[1024,768]{1,0:T(8,128)(2,1)}), bf16[128,768]{1,0:T(8,128)(2,1)}) %reduce-scatter.19.cloned.1.call-update) | async-done | bytes 196624
  411.0 34.3 %reduce-scatter.21.cloned.1.call-done = bf16[128,768]{1,0:T(8,128)(2,1)} async-done(((bf16[1024,768]{1,0:T(8,128)(2,1)}), bf16[128,768]{1,0:T(8,128)(2,1)}) %reduce-scatter.21.cloned.1.call-update) | async-done | bytes 196624
  449.3 5.8 copy.44
  457.6 3.7 convolution_convert_fusion.1
  461.3 3.6 convolution_convert_fusion
  465.0 35.7 %reduce-scatter.23.cloned.1.call-done = bf16[192,2304]{1,0:T(8,128)(2,1)} async-done(((bf16[768,2304]{1,0:T(8,128)(2,1)}), bf16[192,2304]{1,0:T(8,128)(2,1)}) %reduce-scatter.23.cloned.1.call-update) | async-done | bytes 884752
  503.0 29.7 %reduce-scatter.13.cloned.1.call-done = bf16[192,768]{1,0:T(8,128)(2,1)} async-done(((bf16[768,768]{1,0:T(8,128)(2,1)}), bf16[192,768]{1,0:T(8,128)(2,1)}) %reduce-scatter.13.cloned.1.call-update) | async-done | bytes 294928 | tf_op jit(solution)/shard_map/reduce_scatter | solution.py:209
  532.8 60.0 %reduce-scatter.15.cloned.1.call-done = bf16[192,3072]{1,0:T(8,128)(2,1)} async-done(((bf16[768,3072]{1,0:T(8,128)(2,1)}), bf16[192,3072]{1,0:T(8,128)(2,1)}) %reduce-scatter.15.cloned.1.call-update) | async-done | bytes 1179664 | tf_op jit(solution)/shard_map/reduce_scatter | solution.py:221
  592.8 59.8 %reduce-scatter.17.cloned.1.call-done = bf16[768,768]{1,0:T(8,128)(2,1)} async-done(((bf16[3072,768]{1,0:T(8,128)(2,1)}), bf16[768,768]{1,0:T(8,128)(2,1)}) %reduce-scatter.17.cloned.1.call-update) | async-done | bytes 1179664 | tf_op jit(solution)/shard_map/reduce_scatter | solution.py:227
  659.2 16.7 %all-reduce.19 = (bf16[768]{0:T(1024)(128)(2,1)}, bf16[768]{0:T(1024)(128)(2,1)}, bf16[768]{0:T(1024)(128)(2,1)}, bf16[768]{0:T(1024)(128)(2,1)}, bf16[768]{0:T(...) all-reduce(bf16[768]{0:T(1024)(128)(2,1)} %dynamic-update-slice.7, ...), channel_id=1, replica_groups=mesh['shard'=4,'ctx'=8] {'shard'}, use_global_device_ids=true, to_apply=%add.7 | all-reduce | flops 9984 | bytes 39936
  686.7 15.6 %all-reduce.17 = (bf16[192]{0:T(256)(128)(2,1)}, bf16[192]{0:T(256)(128)(2,1)}, bf16[192]{0:T(256)(128)(2,1)}, bf16[192]{0:T(256)(128)(2,1)}, bf16[192]{0:T(256)...) all-reduce(bf16[192]{0:T(256)(128)(2,1)} %dynamic-slice.9, ...), channel_id=1, replica_groups=mesh['shard'=4,'ctx'=8] {'ctx'}, use_global_device_ids=true, to_apply=%region_21.22 | all-reduce | flops 2304 | bytes 9216 | tf_op jit(solution)/shard_map/psum | solution.py:242
  718.3 28.3 %all-reduce.23.cloned.1.call-done = (bf16[192,2304]{0,1:T(8,128)(2,1)}, bf16[192,768]{1,0:T(8,128)(2,1)}, bf16[192,3072]{1,0:T(8,128)(2,1)}, bf16[768,768]{1,0:T(8,128)(2,1)}) async-done(((bf16[192,2304]{0,1:T(8,128)(2,1)}, bf16[192,768]{1,0:T(8,128)(2,1)}, bf16[192,3072]{1,0:T(8,128)(2,1)}, bf16[768,768]{1,0:T(8,128)(2,1)}), (bf16[192,2304]{0,1:T(8,128)(2,1)}, bf16[192,768]{1,0:T(8,128)(2,1)}, ...) | async-done | bytes 3538960 | tf_op jit(solution)/shard_map/psum | solution.py:241
  (325 shorter events, 226.3 us)
Async XLA Ops:
  7.2 52.7 %all-gather.8.cloned.1.call-start = ((), (), s32[]{:S(2)}) async-start(), calls=%async_computation.6 | async-start | bytes 4423680 | tf_op jit(solution)/shard_map/all_gather | solution.py:60
  7.9 83.3 %all-gather.10.cloned.1.call-start = ((), (), s32[]{:S(2)}) async-start(), calls=%async_computation.7 | async-start | bytes 1769472 | tf_op jit(solution)/shard_map/all_gather | solution.py:101
  63.9 55.3 %all-gather.12.cloned.1.call-start = ((), (), s32[]{:S(2)}) async-start(), calls=%async_computation.8 | async-start | bytes 1769472 | tf_op jit(solution)/shard_map/all_gather | solution.py:100
  64.7 110.5 %all-gather.14.cloned.1.call-start = ((), (), s32[]{:S(2)}) async-start(), calls=%async_computation.9 | async-start | bytes 1474560 | tf_op jit(solution)/shard_map/all_gather | solution.py:63
  65.3 140.8 %all-gather.16.cloned.1.call-start = ((), (), s32[]{:S(2)}) async-start(), calls=%async_computation.10 | async-start | bytes 5898240 | tf_op jit(solution)/shard_map/all_gather | solution.py:67
  65.9 198.8 %all-gather.18.cloned.1.call-start = ((), (), s32[]{:S(2)}) async-start(), calls=%async_computation.11 | async-start | bytes 5898240 | tf_op jit(solution)/shard_map/all_gather | solution.py:69
  66.5 343.5 %reduce-scatter.19.cloned.1.call-start = ((), (), s32[]{:S(2)}) async-start(), calls=%async_computation.15 | async-start | bytes 1769472
  119.3 55.9 %copy-start.5 = (bf16[1,128,768]{2,1,0:T(8,128)(2,1)S(1)}, bf16[1,128,768]{2,1,0:T(8,128)(2,1)}, u32[]{:S(2)}) copy-start(bf16[1,128,768]{2,1,0:T(8,128)(2,1)} %param.20) | copy-start | bytes 589828
  175.2 38.5 %copy-start.9 = (bf16[12,64,128]{2,1,0:T(8,128)(2,1)}, bf16[12,64,128]{2,1,0:T(8,128)(2,1)S(1)}, u32[]{:S(2)}) copy-start(bf16[12,64,128]{2,1,0:T(8,128)(2,1)S(1)} %convert_element_type.205) | copy-start | bytes 589828
  177.2 98.2 %copy-start.16 = (f32[128]{0:T(128)}, f32[128]{0:T(128)S(1)}, u32[]{:S(2)}) copy-start(f32[128]{0:T(128)S(1)} %add_rsqrt_fusion.1) | copy-start | bytes 1540
  268.1 7.3 copy-start.18
  268.3 7.1 copy-start.21
  279.3 175.9 %copy-start.2 = (f32[128,768]{1,0:T(8,128)}, f32[128,768]{1,0:T(8,128)S(1)}, u32[]{:S(2)}) copy-start(f32[128,768]{1,0:T(8,128)S(1)} %get-tuple-element.291) | copy-start | bytes 1179652
  375.6 69.7 %reduce-scatter.21.cloned.1.call-start = ((), (), s32[]{:S(2)}) async-start(), calls=%async_computation.16 | async-start | bytes 1769472
  378.3 122.4 %reduce-scatter.23.cloned.1.call-start = ((), (), s32[]{:S(2)}) async-start(), calls=%async_computation.17 | async-start | bytes 4423680
  379.3 70.0 %copy-start.8 = (bf16[12,64,128]{2,1,0:T(8,128)(2,1)}, bf16[12,64,128]{2,1,0:T(8,128)(2,1)S(1)}, u32[]{:S(2)}) copy-start(bf16[12,64,128]{2,1,0:T(8,128)(2,1)S(1)} %get-tuple-element.298) | copy-start | bytes 589828
  411.0 38.3 %copy-start.6 = (bf16[768,128]{1,0:T(8,128)(2,1)}, bf16[768,128]{1,0:T(8,128)(2,1)S(1)}, u32[]{:S(2)}) copy-start(bf16[768,128]{1,0:T(8,128)(2,1)S(1)} %copy.41) | copy-start | bytes 589828
  455.1 77.6 %reduce-scatter.13.cloned.1.call-start = ((), (), s32[]{:S(2)}) async-start(), calls=%async_computation.12 | async-start | bytes 1474560 | tf_op jit(solution)/shard_map/reduce_scatter | solution.py:209
  457.5 135.3 %reduce-scatter.15.cloned.1.call-start = ((), (), s32[]{:S(2)}) async-start(), calls=%async_computation.13 | async-start | bytes 5898240 | tf_op jit(solution)/shard_map/reduce_scatter | solution.py:221
  461.3 191.4 %reduce-scatter.17.cloned.1.call-start = ((), (), s32[]{:S(2)}) async-start(), calls=%async_computation.14 | async-start | bytes 5898240 | tf_op jit(solution)/shard_map/reduce_scatter | solution.py:227
  464.9 281.7 %all-reduce.23.cloned.1.call-start = ((), (), s32[]{:S(2)}) async-start(), calls=%async_computation.18 | async-start | bytes 7667712 | tf_op jit(solution)/shard_map/psum | solution.py:241
  652.6 6.6 copy-start.20
  652.6 60.5 %copy-start.19 = (f32[128]{0:T(128)S(1)}, f32[128]{0:T(128)}, u32[]{:S(2)}) copy-start(f32[128]{0:T(128)} %copy-done.18) | copy-start | bytes 1540
  652.6 62.3 %copy-start = (bf16[768,2304]{1,0:T(8,128)(2,1)S(1)}, bf16[768,2304]{1,0:T(8,128)(2,1)}, u32[]{:S(2)}) copy-start(bf16[768,2304]{1,0:T(8,128)(2,1)} %all-gather.8.cloned.1.call-done) | copy-start | bytes 10616836
  (15 other events, 45.1 us)
Sparse Core Ops, SparseCore 0:
  9.8 49.9 all-gather.7
  64.0 27.0 all-gather.9
  93.3 25.8 all-gather.11
  121.0 26.3 all-gather.13
  149.1 56.9 all-gather.15
  207.7 56.9 all-gather.17
  375.7 34.1 reduce-scatter.18
  412.8 32.5 reduce-scatter.20
  455.2 45.4 reduce-scatter.22
  504.1 28.6 reduce-scatter.12
  535.8 56.9 reduce-scatter.14
  595.6 56.9 reduce-scatter.16
  655.8 90.7 all-reduce.22
where the time goes:
time: 764 us; the launch traced here: 760 us
  waiting for transfers between devices  431 us (56%)
  matrix products  140 us (18%)
  local copies, waits for them, and re-layouts  66.7 us (9%)
  blocking collectives  58.9 us (8%)
  other arithmetic  46.2 us (6%)
  between operations  16.2 us (2%)
    dot_general x94, matrix products, contract_dims(): lax.dot_general(left, right, (((left_dim,), (right_dim,)), ((), ())), pre...  129 us
    unnamed x16, waiting for transfers between devices  103 us
    reduce_scatter x1, waiting for transfers between devices, local(): lax.psum_scatter(grads[7].astype(jnp.bfloat16), 'shard', scatter_dimensio...  60 us
    reduce_scatter x1, waiting for transfers between devices, local(): lax.psum_scatter(grads[9].astype(jnp.bfloat16), 'shard', scatter_dimensio...  59.8 us
    all_gather x1, waiting for transfers between devices, local(): lax.all_gather(w_down, 'shard', axis=0, tiled=True)  51 us
    unnamed x86, local copies, waits for them, and re-layouts  37.9 us
    unnamed x2, blocking collectives  35 us
    reduce_scatter x1, waiting for transfers between devices, local(): lax.psum_scatter(grads[3].astype(jnp.bfloat16), 'shard', scatter_dimensio...  29.7 us
  transfers between devices with their start and end apart: 13, of which 12 were waited for; matrix products, arithmetic and copies ran while one was open for 16% of the time, Pallas kernels for 0%

commit v1 on v0

--- a/solution.py
+++ b/solution.py
@@ -6,6 +6,28 @@
 
 HEADS = 12
 EPS = 1e-06
+
+
+def in_order(tiles, dim):
+    dims = list(tiles.shape[1:])
+    dims[dim] *= tiles.shape[0]
+    return jnp.moveaxis(tiles, 0, dim).reshape(dims)
+
+
+def collected_by_bits(x, axis):
+    peers = lax.axis_size(axis)
+    blocks = x[None]
+    for level in range(peers.bit_length() - 1):
+        apart = 1 << level
+        other = lax.ppermute(blocks, axis, [(i, i ^ apart) for i in range(peers)])
+        both = jnp.stack([blocks, other])
+        upper = lax.axis_index(axis) >> level & 1
+        blocks = jnp.where(upper == 0, both, both[::-1]).reshape(-1, *x.shape)
+    return blocks
+
+
+def gather_by_bits(x, axis, dim):
+    return in_order(collected_by_bits(x, axis), dim)
 
 
 def normalize(z):
@@ -66,7 +88,7 @@
         lax.all_gather(ln1_bias, "shard", axis=0, tiled=True),
         lax.all_gather(w_up, "shard", axis=0, tiled=True),
         lax.all_gather(b_up, "shard", axis=0, tiled=True),
-        lax.all_gather(w_down, "shard", axis=0, tiled=True),
+        gather_by_bits(w_down, "shard", 0),
         lax.all_gather(b_down, "shard", axis=0, tiled=True),
         lax.all_gather(ln2_gain, "shard", axis=0, tiled=True),
         lax.all_gather(ln2_bias, "shard", axis=0, tiled=True),

time: 764 us -> 703 us (0.920)
  waiting for transfers between devices: 431 us -> 360 us
  blocking collectives: 58.9 us -> 111 us
  local copies, waits for them, and re-layouts: 66.7 us -> 31.4 us
    all_gather x1, blocking collectives: 8.3 us -> 62.7 us  [local(): lax.all_gather(b_up, 'shard', axis=0, tiled=True)]
    all_gather x1 -> x0, waiting for transfers between devices: 51 us -> none  [local(): lax.all_gather(w_down, 'shard', axis=0, tiled=True)]
    all_gather x1, waiting for transfers between devices: 28.1 us -> 0.01 us  [local(): lax.all_gather(keys_t, 'ctx', axis=1, tiled=True)]
    ppermute x0 -> x2, waiting for transfers between devices: none -> 26.1 us  [collected_by_bits(): other = lax.ppermute(blocks, axis, [(i, i ^ apart) for i in range(peers)])]
    all_gather x1, waiting for transfers between devices: 28.8 us -> 5.74 us  [local(): lax.all_gather(w_up, 'shard', axis=0, tiled=True)]
    psum x1, waiting for transfers between devices: 28.3 us -> 50.1 us  [local(): lax.psum(pieces[0].astype(jnp.bfloat16), 'ctx').astype(jnp.float32)]
    all_gather x1, waiting for transfers between devices: 16.2 us -> 0.01 us  [local(): lax.all_gather(values_t, 'ctx', axis=1, tiled=True)]
    dynamic_update_slice x12, local copies, waits for them, and re-layouts: 15.4 us -> 0.45 us  [local(): lax.map(head_fwd, (heads_first(query_t), heads_first(all_keys), heads_fir...]
  transfers between devices with their start and end apart: 13 -> 14, of which waited for: 12 -> 10; matrix products, arithmetic and copies ran while one was open for 16% -> 12% of each run, Pallas kernels for 0% -> 0%
where the time goes in v1:
time: 703 us; the launch traced here: 700 us
  waiting for transfers between devices  360 us (51%)
  matrix products  136 us (19%)
  blocking collectives  111 us (16%)
  other arithmetic  39.7 us (6%)
  local copies, waits for them, and re-layouts  31.4 us (4%)
  between operations  16.7 us (2%)
    dot_general x94, matrix products, contract_dims(): lax.dot_general(left, right, (((left_dim,), (right_dim,)), ((), ())), pre...  129 us
    unnamed x15, waiting for transfers between devices  103 us
    all_gather x1, blocking collectives, local(): lax.all_gather(b_up, 'shard', axis=0, tiled=True)  62.7 us
    reduce_scatter x1, waiting for transfers between devices, local(): lax.psum_scatter(grads[9].astype(jnp.bfloat16), 'shard', scatter_dimensio...  60 us
    reduce_scatter x1, waiting for transfers between devices, local(): lax.psum_scatter(grads[7].astype(jnp.bfloat16), 'shard', scatter_dimensio...  59.9 us
    psum x1, waiting for transfers between devices, local(): lax.psum(pieces[0].astype(jnp.bfloat16), 'ctx').astype(jnp.float32)  50.1 us
    unnamed x2, blocking collectives  33.7 us
    reduce_scatter x1, waiting for transfers between devices, local(): lax.psum_scatter(grads[3].astype(jnp.bfloat16), 'shard', scatter_dimensio...  29.9 us
  transfers between devices with their start and end apart: 14, of which 10 were waited for; matrix products, arithmetic and copies ran while one was open for 12% of the time, Pallas kernels for 0%

profile of v1, /device:TPU:0, one launch (start us, length us, event | category | flops | bytes accessed | tf_op | source)
XLA Modules:
  0.0 700.4 jit_solution(10304759340301452412)
XLA Ops:
  15.8 18.3 %all-reduce.20 = (bf16[768]{0:T(1024)(128)(2,1)S(1)}, bf16[768]{0:T(1024)(128)(2,1)S(1)}, bf16[768]{0:T(1024)(128)(2,1)S(1)}, bf16[768]{0:T(1024)(128)(2,1)S(1)}...) all-reduce(bf16[768]{0:T(1024)(128)(2,1)S(1)} %dynamic-update-slice, ...), channel_id=1, replica_groups=mesh['shard'=4,'ctx'=8] {'shard'}, use_global_device_ids=true, to_apply=%add.1 | all-reduce | flops 5376 | bytes 21504
  34.1 25.7 %all-gather.7.cloned.1.call-done = bf16[768,2304]{1,0:T(8,128)(2,1)} async-done(((bf16[192,2304]{1,0:T(8,128)(2,1)}), bf16[768,2304]{1,0:T(8,128)(2,1)}) %all-gather.7.cloned.1.call-update) | async-done | bytes 3538960 | tf_op jit(solution)/shard_map/all_gather | solution.py:82
  59.8 3.1 fusion.73
  66.3 26.1 %collective-permute-done = bf16[1,768,768]{2,1,0:T(8,128)(2,1)S(1)} collective-permute-done((bf16[1,768,768]{2,1,0:T(8,128)(2,1)S(1)}, bf16[1,768,768]{2,1,0:T(8,128)(2,1)S(1)}, u32[]{:S(2)}, u32[]{:S(2)}) %collective-permute-start) | collective-permute-done | bytes 1179680 | tf_op jit(solution)/shard_map/ppermute | solution.py:22
  96.7 62.7 %all-gather = bf16[4,1,768]{2,1,0:T(2,128)(2,1)S(1)} all-gather(bf16[1,1,768]{2,1,0:T(2,128)(2,1)S(1)} %reshape.178), channel_id=1, replica_groups=mesh['shard'=4,'ctx'=8] {'shard'}, dimensions={0}, use_global_device_ids=true | all-gather | bytes 7680 | tf_op jit(solution)/shard_map/all_gather | solution.py:90
  161.6 3.1 reverse_select_fusion
  164.8 41.1 %while.28 = (s32[]{:T(128)}, f32[12,64,128]{2,1,0:T(8,128)S(1)}, f32[12,128]{1,0:T(8,128)S(1)}, bf16[12,64,1024]{2,1,0:T(8,128)(2,1)}, bf16[12,64,128]{2,1,0:T(8...) while((s32[]{:T(128)}, f32[12,64,128]{2,1,0:T(8,128)S(1)}, ...), condition=%wide.region_3.4_spmd.clone, body=%wide.region_0.3_spmd.clone.sunk | while | flops 34472832 | bytes 1892965 | solution.py:137
  208.5 5.7 all-gather.15.cloned.1.call-done
  214.3 6.0 multiply_convert_fusion
  221.9 4.9 fusion.95
  233.6 78.9 %while.29 = (s32[]{:T(128)}, f32[12,64,128]{2,1,0:T(8,128)S(1)}, bf16[12,64,1024]{2,1,0:T(8,128)(2,1)}, bf16[12,64,1024]{2,1,0:T(8,128)(2,1)}, bf16[12,64,1024]{...) while((s32[]{:T(128)}, f32[12,64,128]{2,1,0:T(8,128)S(1)}, ...), condition=%wide.region_14.15_spmd.clone, body=%wide.region_13.14_spmd.clone.sunk | while | flops 84878336 | bytes 3385469 | solution.py:190
  318.3 31.3 %reduce-scatter.19.cloned.1.call-done = bf16[128,768]{1,0:T(8,128)(2,1)} async-done(((bf16[1024,768]{1,0:T(8,128)(2,1)}), bf16[128,768]{1,0:T(8,128)(2,1)}) %reduce-scatter.19.cloned.1.call-update) | async-done | bytes 196624
  350.7 34.4 %reduce-scatter.21.cloned.1.call-done = bf16[128,768]{1,0:T(8,128)(2,1)} async-done(((bf16[1024,768]{1,0:T(8,128)(2,1)}), bf16[128,768]{1,0:T(8,128)(2,1)}) %reduce-scatter.21.cloned.1.call-update) | async-done | bytes 196624
  389.0 5.8 copy.44
  397.4 3.6 convolution_convert_fusion.1
  401.1 3.6 convolution_convert_fusion
  404.8 35.7 %reduce-scatter.23.cloned.1.call-done = bf16[192,2304]{1,0:T(8,128)(2,1)} async-done(((bf16[768,2304]{1,0:T(8,128)(2,1)}), bf16[192,2304]{1,0:T(8,128)(2,1)}) %reduce-scatter.23.cloned.1.call-update) | async-done | bytes 884752
  442.8 29.9 %reduce-scatter.13.cloned.1.call-done = bf16[192,768]{1,0:T(8,128)(2,1)} async-done(((bf16[768,768]{1,0:T(8,128)(2,1)}), bf16[192,768]{1,0:T(8,128)(2,1)}) %reduce-scatter.13.cloned.1.call-update) | async-done | bytes 294928 | tf_op jit(solution)/shard_map/reduce_scatter | solution.py:231
  472.7 59.9 %reduce-scatter.15.cloned.1.call-done = bf16[192,3072]{1,0:T(8,128)(2,1)} async-done(((bf16[768,3072]{1,0:T(8,128)(2,1)}), bf16[192,3072]{1,0:T(8,128)(2,1)}) %reduce-scatter.15.cloned.1.call-update) | async-done | bytes 1179664 | tf_op jit(solution)/shard_map/reduce_scatter | solution.py:243
  532.6 60.0 %reduce-scatter.17.cloned.1.call-done = bf16[768,768]{1,0:T(8,128)(2,1)} async-done(((bf16[3072,768]{1,0:T(8,128)(2,1)}), bf16[768,768]{1,0:T(8,128)(2,1)}) %reduce-scatter.17.cloned.1.call-update) | async-done | bytes 1179664 | tf_op jit(solution)/shard_map/reduce_scatter | solution.py:249
  595.2 15.4 %all-reduce.19 = (bf16[768]{0:T(1024)(128)(2,1)S(1)}, bf16[768]{0:T(1024)(128)(2,1)S(1)}, bf16[768]{0:T(1024)(128)(2,1)S(1)}, bf16[768]{0:T(1024)(128)(2,1)S(1)}...) all-reduce(bf16[768]{0:T(1024)(128)(2,1)S(1)} %dynamic-update-slice, ...), channel_id=1, replica_groups=mesh['shard'=4,'ctx'=8] {'shard'}, use_global_device_ids=true, to_apply=%add.7 | all-reduce | flops 9984 | bytes 39936
  611.3 15.0 %all-reduce.17 = (bf16[192]{0:T(256)(128)(2,1)S(1)}, bf16[192]{0:T(256)(128)(2,1)S(1)}, bf16[192]{0:T(256)(128)(2,1)S(1)}, bf16[192]{0:T(256)(128)(2,1)S(1)}, bf...) all-reduce(bf16[192]{0:T(256)(128)(2,1)S(1)} %dynamic-slice.9, ...), channel_id=1, replica_groups=mesh['shard'=4,'ctx'=8] {'ctx'}, use_global_device_ids=true, to_apply=%region_21.22 | all-reduce | flops 2304 | bytes 9216 | tf_op jit(solution)/shard_map/psum | solution.py:264
  632.2 4.1 fusion.57
  636.3 50.1 %all-reduce.23.cloned.1.call-done = (bf16[192,2304]{0,1:T(8,128)(2,1)}, bf16[192,768]{1,0:T(8,128)(2,1)}, bf16[192,3072]{1,0:T(8,128)(2,1)}, bf16[768,768]{1,0:T(8,128)(2,1)}) async-done(((bf16[192,2304]{0,1:T(8,128)(2,1)}, bf16[192,768]{1,0:T(8,128)(2,1)}, bf16[192,3072]{1,0:T(8,128)(2,1)}, bf16[768,768]{1,0:T(8,128)(2,1)}), (bf16[192,2304]{0,1:T(8,128)(2,1)}, bf16[192,768]{1,0:T(8,128)(2,1)}, ...) | async-done | bytes 3538960 | tf_op jit(solution)/shard_map/psum | solution.py:263
  (325 shorter events, 178.2 us)
Async XLA Ops:
  7.2 52.7 %all-gather.7.cloned.1.call-start = ((), (), s32[]{:S(2)}) async-start(), calls=%async_computation.6 | async-start | bytes 4423680 | tf_op jit(solution)/shard_map/all_gather | solution.py:82
  7.9 156.8 %all-gather.9.cloned.1.call-start = ((), (), s32[]{:S(2)}) async-start(), calls=%async_computation.7 | async-start | bytes 1769472 | tf_op jit(solution)/shard_map/all_gather | solution.py:123
  63.9 100.8 %all-gather.11.cloned.1.call-start = ((), (), s32[]{:S(2)}) async-start(), calls=%async_computation.8 | async-start | bytes 1769472 | tf_op jit(solution)/shard_map/all_gather | solution.py:122
  64.7 141.2 %all-gather.13.cloned.1.call-start = ((), (), s32[]{:S(2)}) async-start(), calls=%async_computation.9 | async-start | bytes 1474560 | tf_op jit(solution)/shard_map/all_gather | solution.py:85
  64.8 27.6 %collective-permute-start = (bf16[1,768,768]{2,1,0:T(8,128)(2,1)S(1)}, bf16[1,768,768]{2,1,0:T(8,128)(2,1)S(1)}, u32[]{:S(2)}, u32[]{:S(2)}) collective-permute-start(bf16[1,768,768]{2,1,0:T(8,128)(2,1)S(1)} %bitcast.169), channel_id=1, source_target_pairs={{0,8},{8,0},{16,24},{24,16},{1,9},{9,1},{17,25},{25,17},{2,10},{10... | collective-permute-start | bytes 3538952 | tf_op jit(solution)/shard_map/ppermute | solution.py:22
  92.6 4.1 copy-start.17
  94.5 65.0 %collective-permute-start.1 = (bf16[2,768,768]{2,1,0:T(8,128)(2,1)}, bf16[2,768,768]{2,1,0:T(8,128)(2,1)}, u32[]{:S(2)}, u32[]{:S(2)}) collective-permute-start(bf16[2,768,768]{2,1,0:T(8,128)(2,1)} %get-tuple-element.297), channel_id=1, source_target_pairs={{0,16},{8,24},{16,0},{24,8},{1,17},{9,25},{17,1},{25,9},{2,18},{10... | collective-permute-start | bytes 7077896 | tf_op jit(solution)/shard_map/ppermute | solution.py:22
  96.0 118.3 %all-gather.15.cloned.1.call-start = ((), (), s32[]{:S(2)}) async-start(), calls=%async_computation.10 | async-start | bytes 5898240 | tf_op jit(solution)/shard_map/all_gather | solution.py:89
  96.6 253.0 %reduce-scatter.19.cloned.1.call-start = ((), (), s32[]{:S(2)}) async-start(), calls=%async_computation.14 | async-start | bytes 1769472
  164.8 41.8 %copy-start.3 = (bf16[1,128,768]{2,1,0:T(8,128)(2,1)S(1)}, bf16[1,128,768]{2,1,0:T(8,128)(2,1)}, u32[]{:S(2)}) copy-start(bf16[1,128,768]{2,1,0:T(8,128)(2,1)} %param.20) | copy-start | bytes 589828
  205.9 14.4 %copy-start.8 = (bf16[12,64,128]{2,1,0:T(8,128)(2,1)}, bf16[12,64,128]{2,1,0:T(8,128)(2,1)S(1)}, u32[]{:S(2)}) copy-start(bf16[12,64,128]{2,1,0:T(8,128)(2,1)S(1)} %convert_element_type.205) | copy-start | bytes 589828
  206.5 13.7 %slice-start = ((s8[4718592]{0:T(1024)(128)(4,1)}), s8[524288]{0:T(1024)(128)(4,1)S(1)}, s32[]{:S(2)}) async-start(s8[4718592]{0:T(1024)(128)(4,1)} %bitcast.153), calls=%async_computation.18 | async-start | bytes 1048576
  214.3 6.0 slice-start.1
  221.7 5.1 slice-start.2
  221.9 4.9 slice-start.3
  315.2 69.9 %reduce-scatter.21.cloned.1.call-start = ((), (), s32[]{:S(2)}) async-start(), calls=%async_computation.15 | async-start | bytes 1769472
  317.8 122.6 %reduce-scatter.23.cloned.1.call-start = ((), (), s32[]{:S(2)}) async-start(), calls=%async_computation.16 | async-start | bytes 4423680
  318.3 70.7 %copy-start.6 = (bf16[12,64,128]{2,1,0:T(8,128)(2,1)}, bf16[12,64,128]{2,1,0:T(8,128)(2,1)S(1)}, u32[]{:S(2)}) copy-start(bf16[12,64,128]{2,1,0:T(8,128)(2,1)S(1)} %get-tuple-element.300) | copy-start | bytes 589828
  394.8 77.9 %reduce-scatter.13.cloned.1.call-start = ((), (), s32[]{:S(2)}) async-start(), calls=%async_computation.11 | async-start | bytes 1474560 | tf_op jit(solution)/shard_map/reduce_scatter | solution.py:231
  397.4 135.2 %reduce-scatter.15.cloned.1.call-start = ((), (), s32[]{:S(2)}) async-start(), calls=%async_computation.12 | async-start | bytes 5898240 | tf_op jit(solution)/shard_map/reduce_scatter | solution.py:243
  401.1 191.5 %reduce-scatter.17.cloned.1.call-start = ((), (), s32[]{:S(2)}) async-start(), calls=%async_computation.13 | async-start | bytes 5898240 | tf_op jit(solution)/shard_map/reduce_scatter | solution.py:249
  404.7 281.7 %all-reduce.23.cloned.1.call-start = ((), (), s32[]{:S(2)}) async-start(), calls=%async_computation.17 | async-start | bytes 7667712 | tf_op jit(solution)/shard_map/psum | solution.py:263
  592.6 39.7 %copy-start.5 = (bf16[768,128]{1,0:T(8,128)(2,1)S(1)}, bf16[768,128]{1,0:T(8,128)(2,1)}, u32[]{:S(2)}) copy-start(bf16[768,128]{1,0:T(8,128)(2,1)} %copy-done.4) | copy-start | bytes 589828
  592.6 39.7 %copy-start.7 = (bf16[12,64,128]{2,1,0:T(8,128)(2,1)S(1)}, bf16[12,64,128]{2,1,0:T(8,128)(2,1)}, u32[]{:S(2)}) copy-start(bf16[12,64,128]{2,1,0:T(8,128)(2,1)} %copy-done.6) | copy-start | bytes 589828
  (13 other events, 24.3 us)
Sparse Core Ops, SparseCore 0:
  9.8 49.9 all-gather.6
  64.1 27.0 all-gather.8
  93.3 25.7 all-gather.10
  120.9 34.6 all-gather.12
  157.3 56.9 all-gather.14
  315.3 34.2 reduce-scatter.18
  352.4 32.5 reduce-scatter.20
  394.9 45.4 reduce-scatter.22
  444.0 28.6 reduce-scatter.12
  475.5 56.9 reduce-scatter.14
  535.6 56.9 reduce-scatter.16
  595.6 90.7 all-reduce.22
